TPU v7x, 32 devices: a whole 2x2x4 slice. The times are simulated.
32 devices in a mesh: ctx: 4 (over x, core), dp: 2 (over y), tp: 4 (over z).
Axes of the slice: x: 2, y: 2, z: 4, core: 2. Of those that a mesh axis runs over, the one named last changes fastest.
Arguments:
- token_ids: int32 [4, 4], replicated, may hold values from 0 to 50279
- decode_prompt: int32 [4], replicated, may hold values from 0 to 3, as said below
- embedding: bfloat16 [50280, 4096], P('dp', ('ctx', 'tp')), may hold values from -6 to 6
- norm_gain: float32 [4096], replicated, may hold values from 0.1 to 1.9
- w_zx: bfloat16 [2, 128, 64, 4096], P(None, ('tp', 'ctx')), may hold values from -0.09375 to 0.09375
- w_bcdt: bfloat16 [4096, 384], P(None, ('ctx', 'tp')), may hold values from -0.09375 to 0.09375
- conv_x_weight: float32 [4, 128, 64], P(None, ('tp', 'ctx')), may hold values from -3 to 3
- conv_x_bias: float32 [128, 64], P(('tp', 'ctx')), may hold values from -3 to 3
- conv_bc_weight: float32 [4, 256], replicated, may hold values from -3 to 3
- conv_bc_bias: float32 [256], replicated, may hold values from -3 to 3
- dt_bias: float32 [128], P(('tp', 'ctx')), may hold values from -4 to -1
- a_log: float32 [128], P(('tp', 'ctx')), may hold values from 0 to 2.7
- d_skip: float32 [128], P(('tp', 'ctx')), may hold values from 0.5 to 1.5
- gate_norm_gain: float32 [128, 64], P(('tp', 'ctx')), may hold values from 0.1 to 1.9
- w_out: bfloat16 [128, 64, 4096], P(('tp', 'ctx')), may hold values from -0.0625 to 0.0625
- state_parts: bfloat16 [4, 4, 128, 64, 128], P('ctx', 'dp', 'tp'), may hold values from -6 to 6
- seg_rate: float32 [4, 4, 128], P('ctx', 'dp', 'tp'), may hold values from 0 to 4
- x_tail: bfloat16 [4, 3, 128, 64], P('dp', None, ('tp', 'ctx')), may hold values from -6 to 6
- bc_tail: bfloat16 [4, 3, 256], P('dp'), may hold values from -6 to 6
Outputs:
- mixer_out: bfloat16 [4, 4, 4096], P(None, 'dp', ('ctx', 'tp'))
- final_state: float32 [4, 128, 64, 128], P('dp', ('tp', 'ctx'))
Inputs may be any that keep to these rules, and one draw needn't show every extreme that they name: decode_prompt is a permutation of the prompts; slot s is decoded by dp group s // 2, and prompt q is held by dp group q // 2; the 2 prompts held by one dp group are decoded by 2 different dp groups.
All inputs are finite; a program needn't handle non-finite values.
Results may differ from a plain program's by a relative error of at most 0.02.
Values may be sent and summed in bfloat16 or wider, within the bound.
A program may use at most 64 MiB of HBM per device.

v0:
```python
import jax
import jax.numpy as jnp
from jax import lax
from jax.sharding import PartitionSpec as P

HEADS = 128
HEAD_DIM = 64
epsilon = 1e-05


def entering(shard, axis, combine, identity):
    count, here = (lax.axis_size(axis), lax.axis_index(axis))
    everything = lax.all_gather(shard, axis)
    start = jnp.broadcast_to(jnp.asarray(identity, shard.dtype), shard.shape)

    def step(k, before):
        at = count - 1 - k
        reached = at > here
        new = combine(before, everything[at])
        return jnp.where(reached, new, before)

    return lax.fori_loop(0, count, step, start)


def rms_scale(values, gain):
    return values * lax.rsqrt(jnp.mean(values * values, axis=-1, keepdims=True) + epsilon) * gain


def select_rows(picker, values):
    return jnp.tensordot(picker, values, axes=1, precision=lax.Precision.HIGHEST)


def add_rates(earlier, later_one):
    return earlier + later_one


def per_device(
    token_ids,
    decode_prompt,
    embedding,
    norm_gain,
    w_zx,
    w_bcdt,
    conv_x_weight,
    conv_x_bias,
    conv_bc_weight,
    conv_bc_bias,
    dt_bias,
    a_log,
    d_skip,
    gate_norm_gain,
    w_out,
    state_parts,
    seg_rate,
    x_tail,
    bc_tail,
):
    group = lax.axis_index("dp")
    local_count = state_parts.shape[1]
    slot_count = decode_prompt.shape[0]
    head_count = w_zx.shape[1]
    state_width = conv_bc_bias.shape[0] // 2
    after_rates = entering(seg_rate, "ctx", add_rates, jnp.zeros_like(seg_rate))
    seg_weight = jnp.exp(-after_rates[0])
    scaled = seg_weight[:, :, None, None] * state_parts[0].astype(jnp.float32)
    channel_sums = lax.psum_scatter(
        scaled.astype(jnp.bfloat16), "ctx", scatter_dimension=2, tiled=True
    ).astype(jnp.float32)
    combined = lax.all_to_all(
        channel_sums.astype(jnp.bfloat16), "ctx", split_axis=1, concat_axis=2, tiled=True
    ).astype(channel_sums.dtype)
    tails_x = x_tail.astype(jnp.float32)
    tails_bc = bc_tail.astype(jnp.float32)
    own_slots = lax.dynamic_slice_in_dim(decode_prompt, group * local_count, local_count)
    prompt_ids = jnp.arange(slot_count, dtype=jnp.int32)
    every_state, every_x, every_bc = (
        lax.all_gather(combined.astype(jnp.bfloat16), "dp", axis=0, tiled=True).astype(
            combined.dtype
        ),
        lax.all_gather(tails_x.astype(jnp.bfloat16), "dp", axis=0, tiled=True).astype(
            tails_x.dtype
        ),
        lax.all_gather(tails_bc.astype(jnp.bfloat16), "dp", axis=0, tiled=True).astype(
            tails_bc.dtype
        ),
    )
    picker = (own_slots[:, None] == prompt_ids[None, :]).astype(jnp.float32)
    ssm_state = select_rows(picker, every_state)
    x_window = select_rows(picker, every_x)
    bc_window = select_rows(picker, every_bc)
    vocab_rows = embedding.shape[0]
    holder = (decode_prompt[:, None] == prompt_ids[None, :]).astype(jnp.int32)
    slot_tokens = jnp.sum(token_ids[:, None, :] * holder[None], axis=2)
    offset_tokens = slot_tokens - group * vocab_rows
    inside = (offset_tokens >= 0) & (offset_tokens < vocab_rows)
    looked = jnp.take(embedding, jnp.clip(offset_tokens, 0, vocab_rows - 1), axis=0)
    partial_rows = jnp.where(inside[..., None], looked.astype(jnp.float32), 0.0)
    own_rows = lax.psum_scatter(
        partial_rows.astype(jnp.bfloat16), "dp", scatter_dimension=1, tiled=True
    )
    embedded = lax.all_gather(own_rows, ("ctx", "tp"), axis=2, tiled=True)
    steps_count = embedded.shape[0]
    flat_rows = embedded.reshape(-1, embedded.shape[2]).astype(jnp.float32)
    normed = rms_scale(flat_rows, norm_gain).astype(jnp.bfloat16)
    projected = jnp.einsum("rd,khed->krhe", normed, w_zx, preferred_element_type=jnp.float32)
    projected = projected.reshape(
        2, steps_count, local_count, projected.shape[2], projected.shape[3]
    )
    columns = lax.all_gather(
        jnp.dot(normed, w_bcdt, preferred_element_type=jnp.float32),
        ("ctx", "tp"),
        axis=1,
        tiled=True,
    )
    columns = columns.reshape(steps_count, local_count, -1)
    head_block = lax.axis_index("tp") * lax.axis_size("ctx") + lax.axis_index("ctx")
    head_start = 2 * state_width + head_block * head_count
    dt_raw = lax.dynamic_slice_in_dim(columns, head_start, head_count, 2)
    decay_rate = -jnp.exp(a_log)
    gated_steps = []
    for moment in range(steps_count):
        x_window = jnp.concatenate([x_window, projected[1, moment][:, None]], axis=1)
        bc_window = jnp.concatenate(
            [bc_window, columns[moment, :, None, : 2 * state_width]], axis=1
        )
        x_conv = jax.nn.silu(jnp.einsum("pkhe,khe->phe", x_window, conv_x_weight) + conv_x_bias)
        bc_conv = jax.nn.silu(jnp.einsum("pkn,kn->pn", bc_window, conv_bc_weight) + conv_bc_bias)
        step_size = jax.nn.softplus(dt_raw[moment] + dt_bias)
        retain = jnp.exp(step_size * decay_rate)
        ssm_state = (
            retain[:, :, None, None] * ssm_state
            + (step_size[:, :, None] * x_conv)[:, :, :, None] * bc_conv[:, None, None, :state_width]
        )
        output = (
            jnp.einsum("phen,pn->phe", ssm_state, bc_conv[:, state_width:])
            + d_skip[None, :, None] * x_conv
        )
        gated_steps.append(output * jax.nn.silu(projected[0, moment]))
        x_window = x_window[:, 1:]
        bc_window = bc_window[:, 1:]
    gated_all = jnp.stack(gated_steps)
    local_squares = jnp.sum(gated_all * gated_all, axis=(2, 3))
    total_squares = lax.psum(local_squares, ("ctx", "tp"))
    inverse = lax.rsqrt(total_squares / (HEADS * HEAD_DIM) + epsilon)
    normed_out = (gated_all * inverse[:, :, None, None] * gate_norm_gain).astype(jnp.bfloat16)
    partial_out = jnp.einsum("tphe,hed->tpd", normed_out, w_out, preferred_element_type=jnp.float32)
    outer_sum = lax.psum_scatter(
        partial_out.astype(jnp.bfloat16), "ctx", scatter_dimension=2, tiled=True
    ).astype(jnp.float32)
    mixed = lax.psum_scatter(outer_sum, "tp", scatter_dimension=2, tiled=True)
    return (mixed.astype(jnp.bfloat16), ssm_state)


def solution(mesh):
    return jax.shard_map(
        per_device,
        mesh=mesh,
        in_specs=(
            P(),
            P(),
            P("dp", ("ctx", "tp")),
            P(),
            P(None, ("tp", "ctx"), None, None),
            P(None, ("ctx", "tp")),
            P(None, ("tp", "ctx"), None),
            P(("tp", "ctx"), None),
            P(),
            P(),
            P(("tp", "ctx")),
            P(("tp", "ctx")),
            P(("tp", "ctx")),
            P(("tp", "ctx"), None),
            P(("tp", "ctx"), None, None),
            P("ctx", "dp", "tp", None, None),
            P("ctx", "dp", "tp"),
            P("dp", None, ("tp", "ctx"), None),
            P("dp", None, None),
        ),
        out_specs=(P(None, "dp", ("ctx", "tp")), P("dp", ("tp", "ctx"), None, None)),
        check_vma=False,
    )
```

profile of v0, /device:TPU:0, one launch (start us, length us, event | category | flops | bytes accessed | tf_op | source)
XLA Modules:
  0.0 232.6 jit_solution(4422377353734788636)
XLA Ops:
  7.3 6.4 %all-gather = f32[4,2,32]{2,1,0:T(2,128)S(1)} all-gather(f32[1,2,32]{2,1,0:T(2,128)} %param.37), channel_id=2, replica_groups=mesh['ctx'=4,'dp'=2,'tp'=4] {'ctx'}, dimensions={0}, use_global_device_ids=true | all-gather | bytes 1280 | tf_op jit(solution)/shard_map/all_gather | solution.py:13
  13.7 0.1 while.16
  13.8 0.1 copy.185
  13.9 2.5 %fusion.2 = bf16[2,32,64,128]{3,2,0,1:T(8,128)(2,1)} fusion(bf16[1,2,32,64,128]{4,3,2,1,0:T(8,128)(2,1)} %param.36, f32[2,32]{0,1:T(8,128)S(1)} %copy.185), kind=kLoop, calls=%fused_computation.6 | loop fusion | flops 1572864 | bytes 2097408 | tf_op jit(solution)/shard_map/convert_element_type | solution.py:67
  16.4 0.7 fusion.65
  17.1 0.8 multiply_reduce_fusion.2
  18.0 0.1 reshape.339
  18.1 0.1 copy.177
  18.2 0.1 copy.178
  18.3 6.9 %gather_fusion = bf16[16,256]{1,0:T(8,128)(2,1)S(1)} fusion(bf16[25140,256]{1,0:T(8,128)(2,1)} %param.23, s32[1024]{0:T(1024)S(1)} %pad_clamp_fusion), kind=kCustom, calls=%fused_computation | custom fusion | bytes 16448 | tf_op jit(solution)/shard_map/jit(_take)/gather | solution.py:96
  25.2 0.1 select_convert_fusion
  25.3 5.0 %all-reduce = bf16[4,4,256]{2,0,1:T(4,128)(2,1)S(1)} all-reduce(bf16[4,4,256]{2,0,1:T(4,128)(2,1)S(1)} %select_convert_fusion), channel_id=3, replica_groups=mesh['ctx'=4,'dp'=2,'tp'=4] {'dp'}, use_global_device_ids=true, to_apply=%region_1.2.clone | all-reduce | flops 4096 | bytes 16384
  30.3 1.2 dynamic-slice
  32.2 32.8 %all_gather.21 = bf16[4,2,4096]{2,0,1:T(4,128)(2,1)S(1)} all-gather(bf16[4,2,256]{2,0,1:T(4,128)(2,1)S(1)} %constant_dynamic-slice_fusion), channel_id=1, replica_groups=mesh['ctx'=4,'dp'=2,'tp'=4] {'ctx','tp'}, dimensions={2}, use_global_device_ids=true | all-gather | bytes 69632 | tf_op jit(solution)/shard_map/all_gather | solution.py:101
  65.0 0.1 multiply_reduce_fusion
  65.2 0.7 dynamic_slice.17
  66.0 0.7 exponential_negate_fusion
  66.6 4.6 %all_gather.26 = bf16[4,3,8,64]{3,2,1,0:T(8,128)(2,1)S(1)} all-gather(bf16[2,3,8,64]{3,2,1,0:T(8,128)(2,1)} %param.38), channel_id=1, replica_groups=mesh['ctx'=4,'dp'=2,'tp'=4] {'dp'}, dimensions={0}, use_global_device_ids=true | all-gather | bytes 18432 | tf_op jit(solution)/shard_map/all_gather | solution.py:80
  71.2 0.1 copy.181
  71.3 0.1 rsqrt.15
  71.4 0.1 reshape.335
  71.5 0.2 convolution_bitcast_fusion.2
  71.8 6.8 %convolution_bitcast_fusion.1 = f32[2,8,8,64]{3,1,2,0:T(8,128)S(1)} fusion(bf16[2,8,64,4096]{3,2,1,0:T(8,128)(2,1)} %param.25, f32[8,4096]{1,0:T(8,128)S(1)} %reshape.335, f32[4096]{0:T(1024)S(1)} %copy-done.2, f32[8]{0:T(128)S(1)} %rsqrt.15), kind=kOutput, calls=%fused_computation.9 | convolution fusion | flops 67207168 | bytes 8568864 | tf_op jit(solution)/shard_map/rd,khed->krhe/dot_general | solution.py:105
  78.6 28.9 %all-gather.1 = f32[16,24,8]{1,2,0:T(8,128)S(1)} all-gather(f32[1,24,8]{1,2,0:T(8,128)S(1)} %convolution_bitcast_fusion.2), channel_id=1, replica_groups=mesh['ctx'=4,'dp'=2,'tp'=4] {'ctx','tp'}, dimensions={0}, use_global_device_ids=true | all-gather | bytes 13056 | tf_op jit(solution)/shard_map/all_gather | solution.py:109
  107.6 0.1 reshape.348
  107.7 0.2 fusion.26
  107.9 0.1 multiply_exponential_fusion.3
  108.1 0.1 copy.183
  108.2 0.1 copy.195
  108.3 0.1 copy.198
  108.3 0.1 copy.201
  108.5 0.1 fusion.19
  108.6 0.1 broadcast_multiply_fusion.3
  108.7 0.2 copy.192
  108.8 0.2 copy.197
  109.0 0.2 copy.200
  109.2 0.2 copy.203
  109.3 4.4 %all_gather.27 = bf16[4,3,256]{2,1,0:T(4,128)(2,1)S(1)} all-gather(bf16[2,3,256]{2,1,0:T(4,128)(2,1)S(1)} %copy.193), channel_id=1, replica_groups=mesh['ctx'=4,'dp'=2,'tp'=4] {'dp'}, dimensions={0}, use_global_device_ids=true | all-gather | bytes 9216 | tf_op jit(solution)/shard_map/all_gather | solution.py:83
  113.7 0.2 fusion.55
  114.0 3.4 %all-to-all-start = ((bf16[2,32,16,128]{3,2,0,1:T(8,128)(2,1)}), bf16[2,32,16,128]{3,2,0,1:T(8,128)(2,1)S(1)}, u32[]{:S(2)}, u32[]{:S(2)}) async-start(bf16[2,32,16,128]{3,2,0,1:T(8,128)(2,1)} %reduce-scatter.8.cloned.1.call-done), calls=%async_computation.1 | async-start | bytes 524288 | tf_op jit(solution)/shard_map/all_to_all | solution.py:69
  117.5 5.9 %all-to-all-done = bf16[2,32,16,128]{3,2,0,1:T(8,128)(2,1)S(1)} async-done(((bf16[2,32,16,128]{3,2,0,1:T(8,128)(2,1)}), bf16[2,32,16,128]{3,2,0,1:T(8,128)(2,1)S(1)}, u32[]{:S(2)}, u32[]{:S(2)}) %all-to-all-start) | async-done | bytes 262176 | tf_op jit(solution)/shard_map/all_to_all | solution.py:69
  123.4 8.4 %all_gather.25 = bf16[4,8,64,128]{3,2,1,0:T(8,128)(2,1)S(1)} all-gather(bf16[2,8,64,128]{3,2,1,0:T(8,128)(2,1)S(1)} %bitcast.312), channel_id=1, replica_groups=mesh['ctx'=4,'dp'=2,'tp'=4] {'dp'}, dimensions={0}, use_global_device_ids=true | all-gather | bytes 786432 | tf_op jit(solution)/shard_map/all_gather | solution.py:77
  131.9 3.2 %multiply_add_fusion = (f32[2,8,64,128]{3,0,2,1:T(2,128)S(1)}, bf16[2,8,64,128]{3,0,2,1:T(2,128)(2,1)S(1)}, bf16[2,8,64,128]{3,0,2,1:T(2,128)(2,1)S(1)}, bf16[2,8,64,128]{3,0,2,1:T(2,128)(2,1)S(1)}) fusion(f32[2,128]{1,0:T(2,128)S(1)} %get-tuple-element.228, f32[2,8,64]{0,2,1:T(8,128)S(1)} %copy.203, f32[2,8]{0,1:T(8,128)S(1)} %copy.201, ...), kind=kOutput, calls=%fused_computation.17 | convolution fusion | flops 3014664 | bytes 1855752 | tf_op jit(solution)/shard_map/dot_general | solution.py:30
  135.1 0.3 fusion.81
  135.4 0.3 fusion.4
  135.7 0.3 fusion.6
  136.1 0.3 fusion.8
  136.4 0.1 multiply_bitcast_fusion.3
  136.5 0.1 multiply_reduce_fusion.1
  136.6 0.1 copy.204
  136.7 31.9 %psum.7 = f32[4,2]{0,1:T(2,128)S(1)} all-reduce(f32[4,2]{0,1:T(2,128)S(1)} %copy.204), channel_id=1, replica_groups=mesh['ctx'=4,'dp'=2,'tp'=4] {'ctx','tp'}, use_global_device_ids=true, to_apply=%region_7.8 | all-reduce | flops 8 | bytes 64 | tf_op jit(solution)/shard_map/psum | solution.py:143
  168.6 0.1 copy.205
  168.7 2.9 %fusion = bf16[4,2,4096]{2,0,1:T(4,128)(2,1)S(1)} fusion(bf16[8,64,4096]{2,1,0:T(8,128)(2,1)} %param.35, bf16[4,2,8,64]{3,2,1,0:T(8,128)(2,1)S(1)} %multiply_convert_fusion.1), kind=kOutput, calls=%fused_computation.3 | convolution fusion | flops 33587200 | bytes 4268032 | tf_op jit(solution)/shard_map/tphe,hed->tpd/dot_general | solution.py:146
  171.7 2.9 %copy.279 = bf16[4,2,4096]{0,1,2:T(2,128)(2,1)S(1)} copy(bf16[4,2,4096]{2,0,1:T(4,128)(2,1)S(1)} %fusion) | data formatting | bytes 131072
  174.6 1.8 reshape.378
  176.5 22.4 %reduce-scatter.10.cloned.1.call-done = bf16[1024,8]{1,0:T(8,128)(2,1)} async-done(((bf16[4096,8]{1,0:T(8,128)(2,1)}), bf16[1024,8]{1,0:T(8,128)(2,1)}) %reduce-scatter.10.cloned.1.call-update) | async-done | bytes 16400
  198.9 1.2 reshape.379
  200.1 0.4 copy.280
  200.5 0.5 copy.281
  200.9 1.4 reshape.380
  202.4 22.0 %reduce-scatter.12.cloned.1.call-done = f32[256,8]{1,0:T(8,128)} async-done(((f32[1024,8]{1,0:T(8,128)}), f32[256,8]{1,0:T(8,128)}) %reduce-scatter.12.cloned.1.call-update) | async-done | bytes 8208
  224.4 1.0 reshape.381
  225.4 0.1 copy.282
  225.5 0.6 copy.207
  (64 shorter events, 0.8 us)
Async XLA Ops:
  7.2 64.3 %copy-start = (bf16[4096,24]{0,1:T(8,128)(2,1)S(1)}, bf16[4096,24]{0,1:T(8,128)(2,1)}, u32[]{:S(2)}) copy-start(bf16[4096,24]{0,1:T(8,128)(2,1)} %param.26) | copy-start | bytes 589828
  7.2 64.3 %copy-start.2 = (f32[4096]{0:T(1024)S(1)}, f32[4096]{0:T(1024)}, u32[]{:S(2)}) copy-start(f32[4096]{0:T(1024)} %param.24) | copy-start | bytes 49156
  7.2 106.8 %reduce-scatter.8.cloned.1.call-start = ((), (), s32[]{:S(2)}) async-start(), calls=%async_computation.4 | async-start | bytes 1310720 | tf_op jit(solution)/shard_map/reduce_scatter | solution.py:66
  71.8 36.2 %copy-start.10 = (f32[8]{0:T(128)S(1)}, f32[8]{0:T(128)}, u32[]{:S(2)}) copy-start(f32[8]{0:T(128)} %param.31) | copy-start | bytes 100
  71.8 36.3 %copy-start.7 = (bf16[2,3,256]{2,0,1:T(2,128)(2,1)S(1)}, bf16[2,3,256]{2,0,1:T(2,128)(2,1)}, u32[]{:S(2)}) copy-start(bf16[2,3,256]{2,0,1:T(2,128)(2,1)} %param.39) | copy-start | bytes 9220
  71.8 36.7 %copy-start.4 = (f32[4,8,64]{2,1,0:T(8,128)S(1)}, f32[4,8,64]{2,1,0:T(8,128)}, u32[]{:S(2)}) copy-start(f32[4,8,64]{2,1,0:T(8,128)} %param.27) | copy-start | bytes 24580
  71.8 36.8 %copy-start.3 = (f32[8,64]{1,0:T(8,128)S(1)}, f32[8,64]{1,0:T(8,128)}, u32[]{:S(2)}) copy-start(f32[8,64]{1,0:T(8,128)} %param.28) | copy-start | bytes 6148
  71.8 42.1 %copy-start.6 = (f32[4,256]{1,0:T(4,128)S(1)}, f32[4,256]{1,0:T(4,128)}, u32[]{:S(2)}) copy-start(f32[4,256]{1,0:T(4,128)} %param.29) | copy-start | bytes 12292
  71.8 42.2 %copy-start.8 = (f32[256]{0:T(256)S(1)}, f32[256]{0:T(256)}, u32[]{:S(2)}) copy-start(f32[256]{0:T(256)} %param.30) | copy-start | bytes 3076
  114.0 9.4 %all-to-all-start = ((bf16[2,32,16,128]{3,2,0,1:T(8,128)(2,1)}), bf16[2,32,16,128]{3,2,0,1:T(8,128)(2,1)S(1)}, u32[]{:S(2)}, u32[]{:S(2)}) async-start(bf16[2,32,16,128]{3,2,0,1:T(8,128)(2,1)} %reduce-scatter.8.cloned.1.call-done), calls=%async_computation.1 | async-start | bytes 524288 | tf_op jit(solution)/shard_map/all_to_all | solution.py:69
  117.5 81.4 %reduce-scatter.10.cloned.1.call-start = ((), (), s32[]{:S(2)}) async-start(), calls=%async_computation.5 | async-start | bytes 1310720
  131.9 4.5 %copy-start.9 = (f32[8]{0:T(128)S(1)}, f32[8]{0:T(128)}, u32[]{:S(2)}) copy-start(f32[8]{0:T(128)} %param.33) | copy-start | bytes 100
  131.9 36.8 %copy-start.5 = (f32[8,64]{1,0:T(8,128)S(1)}, f32[8,64]{1,0:T(8,128)}, u32[]{:S(2)}) copy-start(f32[8,64]{1,0:T(8,128)} %param.34) | copy-start | bytes 6148
  135.1 39.5 %copy-start.1 = (f32[2,8,64,128]{3,2,1,0:T(8,128)}, f32[2,8,64,128]{3,2,1,0:T(8,128)S(1)}, u32[]{:S(2)}) copy-start(f32[2,8,64,128]{3,2,1,0:T(8,128)S(1)} %copy.208) | copy-start | bytes 1572868
  176.4 48.0 %reduce-scatter.12.cloned.1.call-start = ((), (), s32[]{:S(2)}) async-start(), calls=%async_computation.6 | async-start | bytes 655360
Sparse Core Ops, SparseCore 0:
  16.5 26.5 reduce-scatter.7
  176.5 22.3 reduce-scatter.9
  202.5 21.8 reduce-scatter.11
where the time goes:
time: 233 us
  blocking collectives  122 us (52%)
  waiting for transfers between devices  50.4 us (22%)
  local copies, waits for them, and re-layouts  20.9 us (9%)
  between operations  14.8 us (6%)
  matrix products  14.7 us (6%)
  other arithmetic  5.73 us (2%)
  starting transfers between devices  3.54 us (2%)
    unnamed x5, waiting for transfers between devices  44.5 us
    all_gather x1, blocking collectives, per_device(): embedded = lax.all_gather(own_rows, ('ctx', 'tp'), axis=2, tiled=True)  32.8 us
    psum x1, blocking collectives, per_device(): total_squares = lax.psum(local_squares, ('ctx', 'tp'))  31.9 us
    all_gather x1, blocking collectives, per_device(): lax.all_gather(jnp.dot(normed, w_bcdt, preferred_element_type=jnp.float32...  28.9 us
    unnamed x36, local copies, waits for them, and re-layouts  11.3 us
    all_gather x1, blocking collectives, per_device(): lax.all_gather(combined.astype(jnp.bfloat16), 'dp', axis=0, tiled=True)  8.41 us
    gather x2, local copies, waits for them, and re-layouts, per_device(): jnp.take(embedding, jnp.clip(offset_tokens, 0, vocab_rows - 1), axis=0)  6.9 us
    dot_general x1, matrix products, per_device(): jnp.einsum('rd,khed->krhe', normed, w_zx, preferred_element_type=jnp.floa...  6.79 us
  transfers between devices with their start and end apart: 4, of which 3 were waited for; matrix products, arithmetic and copies ran while one was open for 9% of the time, Pallas kernels for 0%

commit v1 on v0

--- a/solution.py
+++ b/solution.py
@@ -140,7 +140,7 @@
         bc_window = bc_window[:, 1:]
     gated_all = jnp.stack(gated_steps)
     local_squares = jnp.sum(gated_all * gated_all, axis=(2, 3))
-    total_squares = lax.psum(local_squares, ("ctx", "tp"))
+    total_squares = lax.psum(lax.psum(local_squares, "tp"), "ctx")
     inverse = lax.rsqrt(total_squares / (HEADS * HEAD_DIM) + epsilon)
     normed_out = (gated_all * inverse[:, :, None, None] * gate_norm_gain).astype(jnp.bfloat16)
     partial_out = jnp.einsum("tphe,hed->tpd", normed_out, w_out, preferred_element_type=jnp.float32)

time: 233 us -> 218 us (0.936)
  blocking collectives: 122 us -> 107 us
    psum x1 -> x2, blocking collectives: 31.9 us -> 16.3 us  [per_device(): total_squares = lax.psum(lax.psum(local_squares, 'tp'), 'ctx')]
  transfers between devices with their start and end apart: 4 -> 4, of which waited for: 3 -> 3; matrix products, arithmetic and copies ran while one was open for 9% -> 10% of each run, Pallas kernels for 0% -> 0%
where the time goes in v1:
time: 218 us; the launch traced here: 217 us
  blocking collectives  107 us (49%)
  waiting for transfers between devices  50.3 us (23%)
  local copies, waits for them, and re-layouts  20.9 us (10%)
  between operations  14.9 us (7%)
  matrix products  14.7 us (7%)
  other arithmetic  5.73 us (3%)
  starting transfers between devices  3.54 us (2%)
    unnamed x5, waiting for transfers between devices  44.4 us
    all_gather x1, blocking collectives, per_device(): embedded = lax.all_gather(own_rows, ('ctx', 'tp'), axis=2, tiled=True)  32.8 us
    all_gather x1, blocking collectives, per_device(): lax.all_gather(jnp.dot(normed, w_bcdt, preferred_element_type=jnp.float32...  28.9 us
    psum x2, blocking collectives, per_device(): total_squares = lax.psum(lax.psum(local_squares, 'tp'), 'ctx')  16.3 us
    unnamed x36, local copies, waits for them, and re-layouts  11.3 us
    all_gather x1, blocking collectives, per_device(): lax.all_gather(combined.astype(jnp.bfloat16), 'dp', axis=0, tiled=True)  8.41 us
    gather x2, local copies, waits for them, and re-layouts, per_device(): jnp.take(embedding, jnp.clip(offset_tokens, 0, vocab_rows - 1), axis=0)  6.9 us
    dot_general x1, matrix products, per_device(): jnp.einsum('rd,khed->krhe', normed, w_zx, preferred_element_type=jnp.floa...  6.79 us
  transfers between devices with their start and end apart: 4, of which 3 were waited for; matrix products, arithmetic and copies ran while one was open for 10% of the time, Pallas kernels for 0%

profile of v1, /device:TPU:0, one launch (start us, length us, event | category | flops | bytes accessed | tf_op | source)
XLA Modules:
  0.0 216.9 jit_solution(2263262972092331855)
XLA Ops:
  7.3 6.4 %all-gather = f32[4,2,32]{2,1,0:T(2,128)S(1)} all-gather(f32[1,2,32]{2,1,0:T(2,128)} %param.37), channel_id=2, replica_groups=mesh['ctx'=4,'dp'=2,'tp'=4] {'ctx'}, dimensions={0}, use_global_device_ids=true | all-gather | bytes 1280 | tf_op jit(solution)/shard_map/all_gather | solution.py:13
  13.7 0.1 while.16
  13.8 0.1 copy.185
  13.9 2.5 %fusion.2 = bf16[2,32,64,128]{3,2,0,1:T(8,128)(2,1)} fusion(bf16[1,2,32,64,128]{4,3,2,1,0:T(8,128)(2,1)} %param.36, f32[2,32]{0,1:T(8,128)S(1)} %copy.185), kind=kLoop, calls=%fused_computation.6 | loop fusion | flops 1572864 | bytes 2097408 | tf_op jit(solution)/shard_map/convert_element_type | solution.py:67
  16.4 0.7 fusion.65
  17.1 0.8 multiply_reduce_fusion.2
  18.0 0.1 reshape.339
  18.1 0.1 copy.177
  18.2 0.1 copy.178
  18.3 6.9 %gather_fusion = bf16[16,256]{1,0:T(8,128)(2,1)S(1)} fusion(bf16[25140,256]{1,0:T(8,128)(2,1)} %param.23, s32[1024]{0:T(1024)S(1)} %pad_clamp_fusion), kind=kCustom, calls=%fused_computation | custom fusion | bytes 16448 | tf_op jit(solution)/shard_map/jit(_take)/gather | solution.py:96
  25.3 5.0 %all-reduce = bf16[4,4,256]{2,0,1:T(4,128)(2,1)S(1)} all-reduce(bf16[4,4,256]{2,0,1:T(4,128)(2,1)S(1)} %select_convert_fusion), channel_id=3, replica_groups=mesh['ctx'=4,'dp'=2,'tp'=4] {'dp'}, use_global_device_ids=true, to_apply=%region_1.2.clone | all-reduce | flops 4096 | bytes 16384
  30.3 1.2 dynamic-slice
  32.2 32.8 %all_gather.21 = bf16[4,2,4096]{2,0,1:T(4,128)(2,1)S(1)} all-gather(bf16[4,2,256]{2,0,1:T(4,128)(2,1)S(1)} %constant_dynamic-slice_fusion), channel_id=1, replica_groups=mesh['ctx'=4,'dp'=2,'tp'=4] {'ctx','tp'}, dimensions={2}, use_global_device_ids=true | all-gather | bytes 69632 | tf_op jit(solution)/shard_map/all_gather | solution.py:101
  65.0 0.1 multiply_reduce_fusion
  65.2 0.7 dynamic_slice.17
  66.0 0.7 exponential_negate_fusion
  66.6 4.6 %all_gather.26 = bf16[4,3,8,64]{3,2,1,0:T(8,128)(2,1)S(1)} all-gather(bf16[2,3,8,64]{3,2,1,0:T(8,128)(2,1)} %param.38), channel_id=1, replica_groups=mesh['ctx'=4,'dp'=2,'tp'=4] {'dp'}, dimensions={0}, use_global_device_ids=true | all-gather | bytes 18432 | tf_op jit(solution)/shard_map/all_gather | solution.py:80
  71.2 0.1 copy.181
  71.3 0.1 rsqrt.15
  71.4 0.1 reshape.335
  71.5 0.2 convolution_bitcast_fusion.2
  71.8 6.8 %convolution_bitcast_fusion.1 = f32[2,8,8,64]{3,1,2,0:T(8,128)S(1)} fusion(bf16[2,8,64,4096]{3,2,1,0:T(8,128)(2,1)} %param.25, f32[8,4096]{1,0:T(8,128)S(1)} %reshape.335, f32[4096]{0:T(1024)S(1)} %copy-done.2, f32[8]{0:T(128)S(1)} %rsqrt.15), kind=kOutput, calls=%fused_computation.9 | convolution fusion | flops 67207168 | bytes 8568864 | tf_op jit(solution)/shard_map/rd,khed->krhe/dot_general | solution.py:105
  78.6 28.9 %all-gather.1 = f32[16,24,8]{1,2,0:T(8,128)S(1)} all-gather(f32[1,24,8]{1,2,0:T(8,128)S(1)} %convolution_bitcast_fusion.2), channel_id=1, replica_groups=mesh['ctx'=4,'dp'=2,'tp'=4] {'ctx','tp'}, dimensions={0}, use_global_device_ids=true | all-gather | bytes 13056 | tf_op jit(solution)/shard_map/all_gather | solution.py:109
  107.6 0.1 reshape.348
  107.7 0.2 fusion.26
  107.9 0.1 multiply_exponential_fusion.3
  108.1 0.1 copy.183
  108.2 0.1 copy.195
  108.3 0.1 copy.198
  108.3 0.1 copy.201
  108.5 0.1 fusion.19
  108.6 0.1 broadcast_multiply_fusion.3
  108.7 0.2 copy.192
  108.8 0.2 copy.197
  109.0 0.2 copy.200
  109.2 0.2 copy.203
  109.3 4.4 %all_gather.27 = bf16[4,3,256]{2,1,0:T(4,128)(2,1)S(1)} all-gather(bf16[2,3,256]{2,1,0:T(4,128)(2,1)S(1)} %copy.193), channel_id=1, replica_groups=mesh['ctx'=4,'dp'=2,'tp'=4] {'dp'}, dimensions={0}, use_global_device_ids=true | all-gather | bytes 9216 | tf_op jit(solution)/shard_map/all_gather | solution.py:83
  113.7 0.2 fusion.55
  114.0 3.4 %all-to-all-start = ((bf16[2,32,16,128]{3,2,0,1:T(8,128)(2,1)}), bf16[2,32,16,128]{3,2,0,1:T(8,128)(2,1)S(1)}, u32[]{:S(2)}, u32[]{:S(2)}) async-start(bf16[2,32,16,128]{3,2,0,1:T(8,128)(2,1)} %reduce-scatter.8.cloned.1.call-done), calls=%async_computation.1 | async-start | bytes 524288 | tf_op jit(solution)/shard_map/all_to_all | solution.py:69
  117.5 5.9 %all-to-all-done = bf16[2,32,16,128]{3,2,0,1:T(8,128)(2,1)S(1)} async-done(((bf16[2,32,16,128]{3,2,0,1:T(8,128)(2,1)}), bf16[2,32,16,128]{3,2,0,1:T(8,128)(2,1)S(1)}, u32[]{:S(2)}, u32[]{:S(2)}) %all-to-all-start) | async-done | bytes 262176 | tf_op jit(solution)/shard_map/all_to_all | solution.py:69
  123.4 8.4 %all_gather.25 = bf16[4,8,64,128]{3,2,1,0:T(8,128)(2,1)S(1)} all-gather(bf16[2,8,64,128]{3,2,1,0:T(8,128)(2,1)S(1)} %bitcast.312), channel_id=1, replica_groups=mesh['ctx'=4,'dp'=2,'tp'=4] {'dp'}, dimensions={0}, use_global_device_ids=true | all-gather | bytes 786432 | tf_op jit(solution)/shard_map/all_gather | solution.py:77
  131.9 3.2 %multiply_add_fusion = (f32[2,8,64,128]{3,0,2,1:T(2,128)S(1)}, bf16[2,8,64,128]{3,0,2,1:T(2,128)(2,1)S(1)}, bf16[2,8,64,128]{3,0,2,1:T(2,128)(2,1)S(1)}, bf16[2,8,64,128]{3,0,2,1:T(2,128)(2,1)S(1)}) fusion(f32[2,128]{1,0:T(2,128)S(1)} %get-tuple-element.228, f32[2,8,64]{0,2,1:T(8,128)S(1)} %copy.203, f32[2,8]{0,1:T(8,128)S(1)} %copy.201, ...), kind=kOutput, calls=%fused_computation.17 | convolution fusion | flops 3014664 | bytes 1855752 | tf_op jit(solution)/shard_map/dot_general | solution.py:30
  135.1 0.3 fusion.81
  135.4 0.3 fusion.4
  135.7 0.3 fusion.6
  136.1 0.3 fusion.8
  136.4 0.1 multiply_bitcast_fusion.3
  136.5 0.1 multiply_reduce_fusion.1
  136.6 0.1 copy.204
  136.7 10.6 %psum.14 = f32[4,2]{0,1:T(2,128)S(1)} all-reduce(f32[4,2]{0,1:T(2,128)S(1)} %copy.204), channel_id=1, replica_groups=mesh['ctx'=4,'dp'=2,'tp'=4] {'tp'}, use_global_device_ids=true, to_apply=%region_7.8 | all-reduce | flops 8 | bytes 64 | tf_op jit(solution)/shard_map/psum | solution.py:143
  147.3 5.6 %psum.15 = f32[4,2]{0,1:T(2,128)S(1)} all-reduce(f32[4,2]{0,1:T(2,128)S(1)} %psum.14), channel_id=1, replica_groups=mesh['ctx'=4,'dp'=2,'tp'=4] {'ctx'}, use_global_device_ids=true, to_apply=%region_8.9 | all-reduce | flops 8 | bytes 64 | tf_op jit(solution)/shard_map/psum | solution.py:143
  153.0 0.1 copy.205
  153.1 2.9 %fusion = bf16[4,2,4096]{2,0,1:T(4,128)(2,1)S(1)} fusion(bf16[8,64,4096]{2,1,0:T(8,128)(2,1)} %param.35, bf16[4,2,8,64]{3,2,1,0:T(8,128)(2,1)S(1)} %multiply_convert_fusion.1), kind=kOutput, calls=%fused_computation.3 | convolution fusion | flops 33587200 | bytes 4268032 | tf_op jit(solution)/shard_map/tphe,hed->tpd/dot_general | solution.py:146
  156.0 2.9 %copy.279 = bf16[4,2,4096]{0,1,2:T(2,128)(2,1)S(1)} copy(bf16[4,2,4096]{2,0,1:T(4,128)(2,1)S(1)} %fusion) | data formatting | bytes 131072
  159.0 1.8 reshape.378
  160.8 22.4 %reduce-scatter.10.cloned.1.call-done = bf16[1024,8]{1,0:T(8,128)(2,1)} async-done(((bf16[4096,8]{1,0:T(8,128)(2,1)}), bf16[1024,8]{1,0:T(8,128)(2,1)}) %reduce-scatter.10.cloned.1.call-update) | async-done | bytes 16400
  183.2 1.2 reshape.379
  184.4 0.4 copy.280
  184.8 0.5 copy.281
  185.3 1.4 reshape.380
  186.7 22.0 %reduce-scatter.12.cloned.1.call-done = f32[256,8]{1,0:T(8,128)} async-done(((f32[1024,8]{1,0:T(8,128)}), f32[256,8]{1,0:T(8,128)}) %reduce-scatter.12.cloned.1.call-update) | async-done | bytes 8208
  208.7 1.0 reshape.381
  209.7 0.1 copy.282
  209.8 0.6 copy.207
  (65 shorter events, 0.9 us)
Async XLA Ops:
  7.2 64.3 %copy-start = (bf16[4096,24]{0,1:T(8,128)(2,1)S(1)}, bf16[4096,24]{0,1:T(8,128)(2,1)}, u32[]{:S(2)}) copy-start(bf16[4096,24]{0,1:T(8,128)(2,1)} %param.26) | copy-start | bytes 589828
  7.2 64.3 %copy-start.2 = (f32[4096]{0:T(1024)S(1)}, f32[4096]{0:T(1024)}, u32[]{:S(2)}) copy-start(f32[4096]{0:T(1024)} %param.24) | copy-start | bytes 49156
  7.2 106.8 %reduce-scatter.8.cloned.1.call-start = ((), (), s32[]{:S(2)}) async-start(), calls=%async_computation.4 | async-start | bytes 1310720 | tf_op jit(solution)/shard_map/reduce_scatter | solution.py:66
  71.8 36.2 %copy-start.10 = (f32[8]{0:T(128)S(1)}, f32[8]{0:T(128)}, u32[]{:S(2)}) copy-start(f32[8]{0:T(128)} %param.31) | copy-start | bytes 100
  71.8 36.3 %copy-start.7 = (bf16[2,3,256]{2,0,1:T(2,128)(2,1)S(1)}, bf16[2,3,256]{2,0,1:T(2,128)(2,1)}, u32[]{:S(2)}) copy-start(bf16[2,3,256]{2,0,1:T(2,128)(2,1)} %param.39) | copy-start | bytes 9220
  71.8 36.7 %copy-start.4 = (f32[4,8,64]{2,1,0:T(8,128)S(1)}, f32[4,8,64]{2,1,0:T(8,128)}, u32[]{:S(2)}) copy-start(f32[4,8,64]{2,1,0:T(8,128)} %param.27) | copy-start | bytes 24580
  71.8 36.8 %copy-start.3 = (f32[8,64]{1,0:T(8,128)S(1)}, f32[8,64]{1,0:T(8,128)}, u32[]{:S(2)}) copy-start(f32[8,64]{1,0:T(8,128)} %param.28) | copy-start | bytes 6148
  71.8 42.1 %copy-start.6 = (f32[4,256]{1,0:T(4,128)S(1)}, f32[4,256]{1,0:T(4,128)}, u32[]{:S(2)}) copy-start(f32[4,256]{1,0:T(4,128)} %param.29) | copy-start | bytes 12292
  71.8 42.2 %copy-start.8 = (f32[256]{0:T(256)S(1)}, f32[256]{0:T(256)}, u32[]{:S(2)}) copy-start(f32[256]{0:T(256)} %param.30) | copy-start | bytes 3076
  114.0 9.4 %all-to-all-start = ((bf16[2,32,16,128]{3,2,0,1:T(8,128)(2,1)}), bf16[2,32,16,128]{3,2,0,1:T(8,128)(2,1)S(1)}, u32[]{:S(2)}, u32[]{:S(2)}) async-start(bf16[2,32,16,128]{3,2,0,1:T(8,128)(2,1)} %reduce-scatter.8.cloned.1.call-done), calls=%async_computation.1 | async-start | bytes 524288 | tf_op jit(solution)/shard_map/all_to_all | solution.py:69
  117.5 65.8 %reduce-scatter.10.cloned.1.call-start = ((), (), s32[]{:S(2)}) async-start(), calls=%async_computation.5 | async-start | bytes 1310720
  131.9 4.5 %copy-start.9 = (f32[8]{0:T(128)S(1)}, f32[8]{0:T(128)}, u32[]{:S(2)}) copy-start(f32[8]{0:T(128)} %param.33) | copy-start | bytes 100
  131.9 21.2 %copy-start.5 = (f32[8,64]{1,0:T(8,128)S(1)}, f32[8,64]{1,0:T(8,128)}, u32[]{:S(2)}) copy-start(f32[8,64]{1,0:T(8,128)} %param.34) | copy-start | bytes 6148
  135.1 23.9 %copy-start.1 = (f32[2,8,64,128]{3,2,1,0:T(8,128)}, f32[2,8,64,128]{3,2,1,0:T(8,128)S(1)}, u32[]{:S(2)}) copy-start(f32[2,8,64,128]{3,2,1,0:T(8,128)S(1)} %copy.208) | copy-start | bytes 1572868
  160.8 47.9 %reduce-scatter.12.cloned.1.call-start = ((), (), s32[]{:S(2)}) async-start(), calls=%async_computation.6 | async-start | bytes 655360
Sparse Core Ops, SparseCore 0:
  16.5 26.5 reduce-scatter.7
  160.9 22.2 reduce-scatter.9
  186.8 21.8 reduce-scatter.11
